TPU v7x, 32 devices: a whole 2x2x4 slice. The times are simulated.
32 devices in a mesh: pop: 8 (over z, x), mp: 4 (over y, core).
Axes of the slice: x: 2, y: 2, z: 4, core: 2. Of those that a mesh axis runs over, the one named last changes fastest.
Arguments:
- context: bfloat16 [3072, 5120], P('pop', 'mp'), may hold values from -9 to 9
- out_weight: bfloat16 [5120, 5120], P('mp'), may hold values from -0.078125 to 0.078125
- residual: bfloat16 [3072, 5120], P('pop', 'mp'), may hold values from -6 to 6
- target: bfloat16 [3072, 5120], P('pop', 'mp'), may hold values from -9 to 9
- norm_gain: float32 [5120], replicated, may hold values from 0.5 to 1.5
- left_factors: bfloat16 [128, 5120], P('pop'), may hold values from -6 to 6
- right_factors: bfloat16 [128, 5120], P('pop'), may hold values from -8 to 8
- member_ranks: int32 [128], P('pop'), may hold values from 0 to 127, each once
Outputs:
- update: float32 [5120, 5120], P('pop', 'mp')
- fitness: float32 [128], P('pop')
- base: float32 [3072, 5120], P('pop', 'mp')
Inputs may be any that keep to these rules, and one draw needn't show every extreme that they name: `member_ranks`: each number from 0 to 127 appears exactly once.
All inputs are finite; a program needn't handle non-finite values.
Results may differ from a plain program's by a relative error of at most 0.0095.
Values may be sent and summed in bfloat16 or wider, within the bound.
A program may use at most 64 MiB of HBM per device.

v0:
```python
import math
import jax
import jax.numpy as jnp
from jax import lax
from jax.sharding import PartitionSpec as P

SIGMA = 1.0
EPSILON = 1e-06


def error_sums(stream, lifted, right_rows, gain_part, target_rows, inverse):
    hidden = stream[:, None, :] + lifted[:, :, None] * right_rows[None, :, :]
    differ = gain_part * hidden * inverse[:, :, None] - target_rows[:, None, :]
    return jnp.sum(differ * differ, axis=(0, 2))


def utility(member_ranks, count_all):
    levels = jnp.arange(count_all).astype(jnp.float32)
    ceiling = math.log(count_all / 2 + 1)
    baseline = jnp.maximum(0.0, ceiling - jnp.log(levels + 1.0))
    shaped = jnp.maximum(0.0, ceiling - jnp.log(member_ranks.astype(jnp.float32) + 1.0))
    return shaped / jnp.sum(baseline) - 1.0 / count_all


def shards(
    context, out_weight, residual, target, norm_gain, left_factors, right_factors, member_ranks
):
    tok_count = context.shape[0]
    shard_width = context.shape[1]
    full_width = out_weight.shape[1]
    factor = SIGMA / math.sqrt(full_width)
    offset = lax.axis_index("mp") * shard_width
    left_cols = lax.dynamic_slice_in_dim(left_factors, offset, shard_width, 1)
    right_cols = lax.dynamic_slice_in_dim(right_factors, offset, shard_width, 1)
    partial_value = jnp.dot(context, out_weight, preferred_element_type=jnp.float32)
    projected = lax.dot_general(
        context, left_cols, (((1,), (1,)), ((), ())), preferred_element_type=jnp.float32
    )
    summed = lax.psum_scatter(
        partial_value.astype(jnp.bfloat16), "mp", scatter_dimension=1, tiled=True
    ).astype(jnp.float32)
    stream = residual.astype(jnp.float32) + summed
    gain_part = lax.dynamic_slice_in_dim(norm_gain, offset, shard_width, 0)
    factor_f = right_cols.astype(jnp.float32)
    crossed = jnp.dot(stream, factor_f.T, precision=lax.Precision.HIGHEST)
    per_token = jnp.sum(stream * stream, axis=1)
    per_member = jnp.sum(factor_f * factor_f, axis=1)
    projected, crossed, per_token, per_member = lax.psum(
        (projected, crossed, per_token, per_member), "mp"
    )
    lifted = factor * projected
    meansq = (
        per_token[:, None] + 2.0 * lifted * crossed + lifted * lifted * per_member[None, :]
    ) / full_width
    inverse = lax.rsqrt(meansq + EPSILON)
    local_error = error_sums(
        stream, lifted, factor_f, gain_part, target.astype(jnp.float32), inverse
    )
    member_total = lax.psum(local_error, "mp")
    fitness = -member_total / (tok_count * full_width)
    everyone = lax.all_gather(fitness, "pop", axis=0, tiled=True)
    count_all = everyone.shape[0]
    average = jnp.mean(everyone)
    centre = everyone - average
    spread = jnp.sqrt(jnp.mean(centre * centre) + 1e-05)
    weight = utility(member_ranks, count_all) + (fitness - average) / spread / count_all
    weighted = (weight[:, None] * left_factors.astype(jnp.float32)).astype(jnp.bfloat16)
    weighted_rows = lax.all_to_all(weighted, "pop", split_axis=1, concat_axis=0, tiled=True)
    right_all = lax.all_gather(right_cols, "pop", axis=0, tiled=True)
    update = lax.dot_general(
        weighted_rows, right_all, (((0,), (0,)), ((), ())), preferred_element_type=jnp.float32
    ) * (math.sqrt(count_all) / SIGMA)
    return (update, fitness, stream)


def solution(mesh):
    in_specs = (
        P("pop", "mp"),
        P("mp", None),
        P("pop", "mp"),
        P("pop", "mp"),
        P(),
        P("pop", None),
        P("pop", None),
        P("pop"),
    )
    out_specs = (P("pop", "mp"), P("pop"), P("pop", "mp"))
    return jax.shard_map(shards, mesh=mesh, in_specs=in_specs, out_specs=out_specs, check_vma=False)
```

profile of v0, /device:TPU:0, one launch (start us, length us, event | category | flops | bytes accessed | tf_op | source)
XLA Modules:
  0.0 169.2 jit_solution(15076576406600554811)
XLA Ops:
  7.2 0.0 copy-start
  7.2 0.0 copy-start.5
  7.2 0.0 copy-start.2
  7.2 0.0 reduce-scatter.2.cloned.1.call-start
  7.2 1.4 copy-done
  8.7 11.4 %convolution_convert_fusion = bf16[384,5120]{1,0:T(8,128)(2,1)} fusion(bf16[384,1280]{1,0:T(8,128)(2,1)S(1)} %copy-done, bf16[1280,5120]{1,0:T(8,128)(2,1)} %param.9), kind=kOutput, calls=%fused_computation.1 | convolution fusion | flops 5035130880 | bytes 18022400 | tf_op jit(solution)/shard_map/dot_general | solution.py:35
  20.1 0.0 reduce-scatter.2.cloned.1.call-update
  20.1 0.0 copy-start.4
  20.2 0.0 copy-done.2
  20.2 1.4 convert_element_type.33
  21.6 0.8 dynamic_slice.9
  22.4 0.0 copy-done.5
  22.4 0.6 dynamic-slice
  23.6 0.6 maximum_reduce_fusion
  24.2 0.8 fusion.3
  25.0 0.1 multiply_reduce_fusion.2
  25.1 1.1 convolution_bitcast_fusion
  26.2 39.6 %reduce-scatter.2.cloned.1.call-done = bf16[384,1280]{1,0:T(8,128)(2,1)} async-done(((bf16[384,5120]{1,0:T(8,128)(2,1)}), bf16[384,1280]{1,0:T(8,128)(2,1)}) %reduce-scatter.2.cloned.1.call-update) | async-done | bytes 983056 | tf_op jit(solution)/shard_map/reduce_scatter | solution.py:39
  65.8 1.9 %multiply_reduce_fusion.1 = (f32[384]{0:T(512)S(1)}, f32[384,1280]{1,0:T(8,128)S(1)}) fusion(bf16[384,1280]{1,0:T(8,128)(2,1)} %reduce-scatter.2.cloned.1.call-done, bf16[384,1280]{1,0:T(8,128)(2,1)} %param.10), kind=kLoop, calls=%fused_computation.3 | loop fusion | flops 2457216 | bytes 3933696 | tf_op jit(solution)/shard_map/reduce_sum | solution.py:46
  67.7 0.0 copy-start.1
  67.7 1.0 fusion.4
  68.7 10.7 %all-reduce.1 = (f32[384,16]{0,1:T(8,128)S(1)}, f32[384,16]{0,1:T(8,128)S(1)}, f32[16]{0:T(128)S(1)}, f32[384]{0:T(512)S(1)}) all-reduce(f32[384,16]{0,1:T(8,128)S(1)} %fusion.4, f32[384,16]{0,1:T(8,128)S(1)} %convolution_bitcast_fusion, f32[16]{0:T(128)S(1)} %multiply_reduce_fusion.2, ...), channel_id=1, replica_groups=mesh['pop'=8,'mp'=4] {'mp'}, use_global_device_ids=true, to_apply=%region_5.0 | all-reduce | flops 12688 | bytes 101504 | tf_op jit(solution)/shard_map/psum | solution.py:48
  79.4 0.1 broadcast_multiply_fusion
  79.5 0.1 copy.21
  79.6 0.1 copy.22
  79.8 12.8 %multiply_reduce_fusion = f32[16]{0:T(128)S(1)} fusion(f32[384,1280]{1,0:T(8,128)} %convert_element_type.33, f32[384,16]{1,0:T(8,128)S(1)} %copy.22, f32[16,1280]{1,0:T(8,128)S(1)} %get-tuple-element.9, f32[384,16]{1,0:T(8,128)S(1)} %copy.21, f32[384,1280]{1,0:T(8,128)S(1)} %get-tuple-element.12, f32[1280]{0:T(1024)S(1)} %dynamic_slice.9), kind=kLoop, calls=%fused_computation | loop fusion | flops 55050224 | bytes 4068416 | tf_op jit(solution)/shard_map/reduce_sum | solution.py:14
  92.5 5.8 %psum.39 = f32[16]{0:T(128)S(1)} all-reduce(f32[16]{0:T(128)S(1)} %multiply_reduce_fusion), channel_id=1, replica_groups=mesh['pop'=8,'mp'=4] {'mp'}, use_global_device_ids=true, to_apply=%region_9.0 | all-reduce | flops 16 | bytes 128 | tf_op jit(solution)/shard_map/psum | solution.py:59
  98.3 0.1 fusion.2
  98.4 0.0 copy-start.3
  98.4 21.5 %all-reduce = f32[128]{0:T(128)S(1)} all-reduce(f32[128]{0:T(128)S(1)} %get-tuple-element.7), channel_id=1, replica_groups=mesh['pop'=8,'mp'=4] {'pop'}, use_global_device_ids=true, to_apply=%add | all-reduce | flops 128 | bytes 1024
  119.9 0.6 reduce_sum.58
  121.1 0.6 multiply_reduce_fusion.3
  122.4 0.0 copy-done.4
  122.4 0.6 multiply_add_fusion
  123.0 1.0 multiply_convert_fusion
  124.0 0.7 copy.26
  124.7 3.4 %all-to-all-start = ((bf16[16,8,640]{2,0,1:T(8,128)(2,1)}), bf16[16,8,640]{2,0,1:T(8,128)(2,1)S(1)}, u32[]{:S(2)}, u32[]{:S(2)}) async-start(bf16[16,8,640]{2,0,1:T(8,128)(2,1)} %bitcast.16), calls=%async_computation.1 | async-start | bytes 327680 | tf_op jit(solution)/shard_map/all_to_all | solution.py:68
  128.1 31.9 %all_gather.7 = bf16[128,1280]{1,0:T(8,128)(2,1)S(1)} all-gather(bf16[16,1280]{1,0:T(8,128)(2,1)S(1)} %get-tuple-element.10), channel_id=1, replica_groups=mesh['pop'=8,'mp'=4] {'pop'}, dimensions={0}, use_global_device_ids=true | all-gather | bytes 368640 | tf_op jit(solution)/shard_map/all_gather | solution.py:69
  160.0 0.0 all-to-all-done
  160.0 2.3 %convolution_multiply_fusion = f32[640,1280]{1,0:T(8,128)} fusion(bf16[128,640]{1,0:T(8,128)(2,1)S(1)} %bitcast.17, bf16[128,1280]{1,0:T(8,128)(2,1)S(1)} %all_gather.7), kind=kOutput, calls=%fused_computation.2 | convolution fusion | flops 210534400 | bytes 3768320 | tf_op jit(solution)/shard_map/dot_general | solution.py:70
  162.4 0.0 copy-done.1
  162.4 0.0 copy-done.3
  (1 shorter events, 0.0 us)
Async XLA Ops:
  7.2 1.5 copy-start
  7.2 15.2 %copy-start.5 = (u32[32]{0:T(128)S(1)}, u32[32]{0:T(128)}, u32[]{:S(2)}) copy-start(u32[32]{0:T(128)} %constant.48) | copy-start | bytes 388
  7.2 13.0 %copy-start.2 = (bf16[384,1280]{1,0:T(8,128)(2,1)S(1)}, bf16[384,1280]{1,0:T(8,128)(2,1)}, u32[]{:S(2)}) copy-start(bf16[384,1280]{1,0:T(8,128)(2,1)} %param.11) | copy-start | bytes 2949124
  7.2 58.6 %reduce-scatter.2.cloned.1.call-start = ((), (), s32[]{:S(2)}) async-start(), calls=%async_computation.2 | async-start | bytes 4915200 | tf_op jit(solution)/shard_map/reduce_scatter | solution.py:39
  20.1 102.3 %copy-start.4 = (s32[16]{0:T(128)S(1)}, s32[16]{0:T(128)}, u32[]{:S(2)}) copy-start(s32[16]{0:T(128)} %param.15) | copy-start | bytes 196
  67.7 94.7 %copy-start.1 = (f32[384,1280]{1,0:T(8,128)}, f32[384,1280]{1,0:T(8,128)S(1)}, u32[]{:S(2)}) copy-start(f32[384,1280]{1,0:T(8,128)S(1)} %get-tuple-element.12) | copy-start | bytes 5898244
  98.4 64.0 %copy-start.3 = (f32[16]{0:T(128)}, f32[16]{0:T(128)S(1)}, u32[]{:S(2)}) copy-start(f32[16]{0:T(128)S(1)} %get-tuple-element.8) | copy-start | bytes 196
  124.7 35.3 %all-to-all-start = ((bf16[16,8,640]{2,0,1:T(8,128)(2,1)}), bf16[16,8,640]{2,0,1:T(8,128)(2,1)S(1)}, u32[]{:S(2)}, u32[]{:S(2)}) async-start(bf16[16,8,640]{2,0,1:T(8,128)(2,1)} %bitcast.16), calls=%async_computation.1 | async-start | bytes 327680 | tf_op jit(solution)/shard_map/all_to_all | solution.py:68
Sparse Core Ops, SparseCore 0:
  20.3 45.4 reduce-scatter.1
where the time goes:
time: 170 us; the launch traced here: 169 us
  blocking collectives  69.9 us (41%)
  waiting for transfers between devices  39.6 us (23%)
  other arithmetic  20.5 us (12%)
  between operations  16.1 us (9%)
  matrix products  15.9 us (9%)
  local copies, waits for them, and re-layouts  3.75 us (2%)
  starting transfers between devices  3.42 us (2%)
    reduce_scatter x1, waiting for transfers between devices, shards(): lax.psum_scatter(partial_value.astype(jnp.bfloat16), 'mp', scatter_dimens...  39.6 us
    all_gather x1, blocking collectives, shards(): right_all = lax.all_gather(right_cols, 'pop', axis=0, tiled=True)  31.9 us
    unnamed x1, blocking collectives  21.5 us
    reduce_sum x1, other arithmetic, error_sums(): return jnp.sum(differ * differ, axis=(0, 2))  12.8 us
    dot_general x1, matrix products, shards(): jnp.dot(context, out_weight, preferred_element_type=jnp.float32)  11.4 us
    psum x1, blocking collectives, shards(): lax.psum((projected, crossed, per_token, per_member), 'mp')  10.7 us
    psum x1, blocking collectives, shards(): member_total = lax.psum(local_error, 'mp')  5.77 us
  transfers between devices with their start and end apart: 2, of which 1 were waited for; matrix products, arithmetic and copies ran while one was open for 3% of the time, Pallas kernels for 0%

commit v1 on v0

--- a/solution.py
+++ b/solution.py
@@ -66,7 +66,12 @@
     weight = utility(member_ranks, count_all) + (fitness - average) / spread / count_all
     weighted = (weight[:, None] * left_factors.astype(jnp.float32)).astype(jnp.bfloat16)
     weighted_rows = lax.all_to_all(weighted, "pop", split_axis=1, concat_axis=0, tiled=True)
-    right_all = lax.all_gather(right_cols, "pop", axis=0, tiled=True)
+    ring = [right_cols]
+    for hop in range(7):
+        ring.append(lax.ppermute(ring[-1], "pop", [(dev, (dev + 1) % 8) for dev in range(8)]))
+    right_all = jnp.roll(
+        jnp.concatenate(ring[::-1], axis=0), (lax.axis_index("pop") + 1) * ring[0].shape[0], axis=0
+    )
     update = lax.dot_general(
         weighted_rows, right_all, (((0,), (0,)), ((), ())), preferred_element_type=jnp.float32
     ) * (math.sqrt(count_all) / SIGMA)

time: 170 us -> 158 us (0.929)
  blocking collectives: 69.9 us -> 36.8 us
  local copies, waits for them, and re-layouts: 3.75 us -> 13.3 us
  waiting for transfers between devices: 39.6 us -> 46.4 us
  starting transfers between devices: 3.42 us -> 6.46 us
    ppermute x0 -> x7, waiting for transfers between devices: none -> 40.1 us  [shards(): lax.ppermute(ring[-1], 'pop', [(dev, (dev + 1) % 8) for dev in range(8)])]
    reduce_scatter x1, waiting for transfers between devices: 39.6 us -> 0.01 us  [shards(): lax.psum_scatter(partial_value.astype(jnp.bfloat16), 'mp', scatter_dimens...]
    all_gather x1 -> x0, blocking collectives: 31.9 us -> none  [shards(): right_all = lax.all_gather(right_cols, 'pop', axis=0, tiled=True)]
    unnamed x13 -> x28, local copies, waits for them, and re-layouts: 2.04 us -> 11 us
    all_to_all x1, waiting for transfers between devices: 0.01 us -> 6.25 us  [shards(): lax.all_to_all(weighted, 'pop', split_axis=1, concat_axis=0, tiled=True)]
    ppermute x0 -> x7, starting transfers between devices: none -> 3.04 us  [shards(): lax.ppermute(ring[-1], 'pop', [(dev, (dev + 1) % 8) for dev in range(8)])]
    unnamed x1, blocking collectives: 21.5 us -> 19.4 us
  transfers between devices with their start and end apart: 2 -> 9, of which waited for: 1 -> 8; matrix products, arithmetic and copies ran while one was open for 3% -> 10% of each run, Pallas kernels for 0% -> 0%
where the time goes in v1:
time: 158 us; the launch traced here: 157 us
  waiting for transfers between devices  46.4 us (29%)
  blocking collectives  36.8 us (23%)
  other arithmetic  21.4 us (14%)
  matrix products  16.9 us (11%)
  between operations  16.2 us (10%)
  local copies, waits for them, and re-layouts  13.3 us (8%)
  starting transfers between devices  6.46 us (4%)
    ppermute x7, waiting for transfers between devices, shards(): lax.ppermute(ring[-1], 'pop', [(dev, (dev + 1) % 8) for dev in range(8)])  40.1 us
    unnamed x1, blocking collectives  19.4 us
    reduce_sum x1, other arithmetic, error_sums(): return jnp.sum(differ * differ, axis=(0, 2))  13.4 us
    dot_general x1, matrix products, shards(): jnp.dot(context, out_weight, preferred_element_type=jnp.float32)  11.4 us
    unnamed x28, local copies, waits for them, and re-layouts  11 us
    psum x1, blocking collectives, shards(): lax.psum((projected, crossed, per_token, per_member), 'mp')  10.7 us
    psum x1, blocking collectives, shards(): member_total = lax.psum(local_error, 'mp')  6.69 us
    all_to_all x1, waiting for transfers between devices, shards(): lax.all_to_all(weighted, 'pop', split_axis=1, concat_axis=0, tiled=True)  6.25 us
  transfers between devices with their start and end apart: 9, of which 8 were waited for; matrix products, arithmetic and copies ran while one was open for 10% of the time, Pallas kernels for 0%

profile of v1, /device:TPU:0, one launch (start us, length us, event | category | flops | bytes accessed | tf_op | source)
XLA Modules:
  0.0 157.4 jit_solution(14805843502956383771)
XLA Ops:
  7.2 1.1 copy-done
  8.4 11.4 %convolution_convert_fusion = bf16[384,5120]{1,0:T(8,128)(2,1)} fusion(bf16[384,1280]{1,0:T(8,128)(2,1)S(1)} %copy-done, bf16[1280,5120]{1,0:T(8,128)(2,1)} %param.9), kind=kOutput, calls=%fused_computation.1 | convolution fusion | flops 5035130880 | bytes 18022400 | tf_op jit(solution)/shard_map/dot_general | solution.py:35
  19.9 0.8 fusion.5
  20.7 3.0 %collective-permute-start = (bf16[16,1280]{1,0:T(8,128)(2,1)S(1)}, bf16[16,1280]{1,0:T(8,128)(2,1)S(1)}, u32[]{:S(2)}, u32[]{:S(2)}) collective-permute-start(bf16[16,1280]{1,0:T(8,128)(2,1)S(1)} %get-tuple-element.10), channel_id=1, source_target_pairs={{0,4},{4,8},{8,12},{12,16},{16,20},{20,24},{24,28},{28,0},{1,5},{5... | collective-permute-start | bytes 122888 | tf_op jit(solution)/shard_map/ppermute | solution.py:71
  23.7 5.0 %collective-permute-done = bf16[16,1280]{1,0:T(8,128)(2,1)S(1)} collective-permute-done((bf16[16,1280]{1,0:T(8,128)(2,1)S(1)}, bf16[16,1280]{1,0:T(8,128)(2,1)S(1)}, u32[]{:S(2)}, u32[]{:S(2)}) %collective-permute-start) | collective-permute-done | bytes 40992 | tf_op jit(solution)/shard_map/ppermute | solution.py:71
  28.7 6.7 %collective-permute-done.1 = bf16[16,1280]{1,0:T(8,128)(2,1)S(1)} collective-permute-done((bf16[16,1280]{1,0:T(8,128)(2,1)S(1)}, bf16[16,1280]{1,0:T(8,128)(2,1)S(1)}, u32[]{:S(2)}, u32[]{:S(2)}) %collective-permute-start.1) | collective-permute-done | bytes 40992 | tf_op jit(solution)/shard_map/ppermute | solution.py:71
  35.4 6.7 %collective-permute-done.2 = bf16[16,1280]{1,0:T(8,128)(2,1)S(1)} collective-permute-done((bf16[16,1280]{1,0:T(8,128)(2,1)S(1)}, bf16[16,1280]{1,0:T(8,128)(2,1)S(1)}, u32[]{:S(2)}, u32[]{:S(2)}) %collective-permute-start.2) | collective-permute-done | bytes 40992 | tf_op jit(solution)/shard_map/ppermute | solution.py:71
  42.1 6.7 %collective-permute-done.3 = bf16[16,1280]{1,0:T(8,128)(2,1)S(1)} collective-permute-done((bf16[16,1280]{1,0:T(8,128)(2,1)S(1)}, bf16[16,1280]{1,0:T(8,128)(2,1)S(1)}, u32[]{:S(2)}, u32[]{:S(2)}) %collective-permute-start.3) | collective-permute-done | bytes 40992 | tf_op jit(solution)/shard_map/ppermute | solution.py:71
  48.8 7.0 %collective-permute-done.4 = bf16[16,1280]{1,0:T(8,128)(2,1)S(1)} collective-permute-done((bf16[16,1280]{1,0:T(8,128)(2,1)S(1)}, bf16[16,1280]{1,0:T(8,128)(2,1)S(1)}, u32[]{:S(2)}, u32[]{:S(2)}) %collective-permute-start.4) | collective-permute-done | bytes 40992 | tf_op jit(solution)/shard_map/ppermute | solution.py:71
  55.8 1.1 convolution_bitcast_fusion
  57.0 5.6 %collective-permute-done.5 = bf16[16,1280]{1,0:T(8,128)(2,1)S(1)} collective-permute-done((bf16[16,1280]{1,0:T(8,128)(2,1)S(1)}, bf16[16,1280]{1,0:T(8,128)(2,1)S(1)}, u32[]{:S(2)}, u32[]{:S(2)}) %collective-permute-start.5) | collective-permute-done | bytes 40992 | tf_op jit(solution)/shard_map/ppermute | solution.py:71
  62.5 0.1 multiply_reduce_fusion.2
  62.7 0.8 dynamic_slice.13
  63.5 1.4 convert_element_type.33
  64.9 0.6 dynamic-slice
  66.1 0.7 maximum_reduce_fusion
  66.8 2.4 %collective-permute-done.6 = bf16[16,1280]{1,0:T(8,128)(2,1)S(1)} collective-permute-done((bf16[16,1280]{1,0:T(8,128)(2,1)S(1)}, bf16[16,1280]{1,0:T(8,128)(2,1)S(1)}, u32[]{:S(2)}, u32[]{:S(2)}) %collective-permute-start.6) | collective-permute-done | bytes 40992 | tf_op jit(solution)/shard_map/ppermute | solution.py:71
  69.2 0.6 constant_dynamic-update-slice_fusion.15
  69.8 0.6 constant_dynamic-update-slice_fusion.14
  70.5 0.6 constant_dynamic-update-slice_fusion.13
  71.1 0.6 constant_dynamic-update-slice_fusion.12
  71.7 0.6 constant_dynamic-update-slice_fusion.11
  72.3 0.6 constant_dynamic-update-slice_fusion.10
  72.9 0.6 constant_dynamic-update-slice_fusion.9
  73.6 0.6 constant_dynamic-update-slice_fusion.8
  74.2 0.6 constant_dynamic-update-slice_fusion.7
  74.8 0.6 constant_dynamic-update-slice_fusion.6
  75.4 0.6 constant_dynamic-update-slice_fusion.5
  76.0 0.6 constant_dynamic-update-slice_fusion.4
  76.6 0.6 constant_dynamic-update-slice_fusion.3
  77.2 0.6 constant_dynamic-update-slice_fusion.2
  77.9 1.9 %multiply_reduce_fusion.1 = (f32[384]{0:T(512)S(1)}, f32[384,1280]{1,0:T(8,128)S(1)}) fusion(bf16[384,1280]{1,0:T(8,128)(2,1)} %reduce-scatter.2.cloned.1.call-done, bf16[384,1280]{1,0:T(8,128)(2,1)} %param.10), kind=kLoop, calls=%fused_computation.3 | loop fusion | flops 2457216 | bytes 3933696 | tf_op jit(solution)/shard_map/reduce_sum | solution.py:46
  79.8 1.0 fusion.6
  80.8 10.7 %all-reduce.1 = (f32[384,16]{0,1:T(8,128)S(1)}, f32[384,16]{0,1:T(8,128)S(1)}, f32[16]{0:T(128)S(1)}, f32[384]{0:T(512)S(1)}) all-reduce(f32[384,16]{0,1:T(8,128)S(1)} %fusion.6, f32[384,16]{0,1:T(8,128)S(1)} %convolution_bitcast_fusion, f32[16]{0:T(128)S(1)} %multiply_reduce_fusion.2, ...), channel_id=1, replica_groups=mesh['pop'=8,'mp'=4] {'mp'}, use_global_device_ids=true, to_apply=%region_5.0 | all-reduce | flops 12688 | bytes 101504 | tf_op jit(solution)/shard_map/psum | solution.py:48
  91.7 0.1 copy.22
  91.8 13.4 %multiply_reduce_fusion = f32[16]{0:T(128)S(1)} fusion(f32[384,1280]{1,0:T(8,128)} %convert_element_type.33, f32[384,16]{1,0:T(8,128)S(1)} %copy.22, f32[16,1280]{1,0:T(8,128)S(1)} %get-tuple-element.9, f32[384,16]{1,0:T(8,128)S(1)} %copy.21, f32[384,1280]{1,0:T(8,128)S(1)} %get-tuple-element.12, f32[1280]{0:T(1024)S(1)} %dynamic_slice.13), kind=kLoop, calls=%fused_computation | loop fusion | flops 55050224 | bytes 4068416 | tf_op jit(solution)/shard_map/reduce_sum | solution.py:14
  105.2 6.7 %psum.39 = f32[16]{0:T(128)S(1)} all-reduce(f32[16]{0:T(128)S(1)} %multiply_reduce_fusion), channel_id=1, replica_groups=mesh['pop'=8,'mp'=4] {'mp'}, use_global_device_ids=true, to_apply=%region_9.0 | all-reduce | flops 16 | bytes 128 | tf_op jit(solution)/shard_map/psum | solution.py:59
  112.0 19.4 %all-reduce = f32[128]{0:T(128)S(1)} all-reduce(f32[128]{0:T(128)S(1)} %get-tuple-element.7), channel_id=1, replica_groups=mesh['pop'=8,'mp'=4] {'pop'}, use_global_device_ids=true, to_apply=%add | all-reduce | flops 128 | bytes 1024
  131.4 0.6 reduce_sum.58
  132.6 0.6 multiply_reduce_fusion.3
  133.9 0.7 multiply_add_fusion
  134.6 1.0 multiply_convert_fusion
  135.7 0.7 copy.26
  136.3 3.4 %all-to-all-start = ((bf16[16,8,640]{2,0,1:T(8,128)(2,1)}), bf16[16,8,640]{2,0,1:T(8,128)(2,1)S(1)}, u32[]{:S(2)}, u32[]{:S(2)}) async-start(bf16[16,8,640]{2,0,1:T(8,128)(2,1)} %bitcast.15), calls=%async_computation.1 | async-start | bytes 327680 | tf_op jit(solution)/shard_map/all_to_all | solution.py:68
  139.7 0.6 constant_dynamic-update-slice_fusion.1
  140.3 0.6 constant_dynamic-update-slice_fusion
  141.0 6.3 %all-to-all-done = bf16[16,8,640]{2,0,1:T(8,128)(2,1)S(1)} async-done(((bf16[16,8,640]{2,0,1:T(8,128)(2,1)}), bf16[16,8,640]{2,0,1:T(8,128)(2,1)S(1)}, u32[]{:S(2)}, u32[]{:S(2)}) %all-to-all-start) | async-done | bytes 163872 | tf_op jit(solution)/shard_map/all_to_all | solution.py:68
  147.2 3.3 %convolution_multiply_fusion = f32[640,1280]{1,0:T(8,128)} fusion(bf16[128,640]{1,0:T(8,128)(2,1)S(1)} %bitcast.16, bf16[256,1280]{1,0:T(8,128)(2,1)} %constant_dynamic-update-slice_fusion, s32[]{:T(128)S(6)} %select_n.20), kind=kOutput, calls=%fused_computation.2 | convolution fusion | flops 210534400 | bytes 3768324 | tf_op jit(solution)/shard_map/dot_general | solution.py:75
  (24 shorter events, 0.4 us)
Async XLA Ops:
  7.2 1.2 copy-start
  7.2 56.3 %copy-start.2 = (bf16[384,1280]{1,0:T(8,128)(2,1)S(1)}, bf16[384,1280]{1,0:T(8,128)(2,1)}, u32[]{:S(2)}) copy-start(bf16[384,1280]{1,0:T(8,128)(2,1)} %param.11) | copy-start | bytes 2949124
  7.2 70.7 %reduce-scatter.2.cloned.1.call-start = ((), (), s32[]{:S(2)}) async-start(), calls=%async_computation.2 | async-start | bytes 4915200 | tf_op jit(solution)/shard_map/reduce_scatter | solution.py:39
  19.8 45.0 %copy-start.5 = (u32[32]{0:T(128)S(1)}, u32[32]{0:T(128)}, u32[]{:S(2)}) copy-start(u32[32]{0:T(128)} %constant.78) | copy-start | bytes 388
  20.7 8.0 %collective-permute-start = (bf16[16,1280]{1,0:T(8,128)(2,1)S(1)}, bf16[16,1280]{1,0:T(8,128)(2,1)S(1)}, u32[]{:S(2)}, u32[]{:S(2)}) collective-permute-start(bf16[16,1280]{1,0:T(8,128)(2,1)S(1)} %get-tuple-element.10), channel_id=1, source_target_pairs={{0,4},{4,8},{8,12},{12,16},{16,20},{20,24},{24,28},{28,0},{1,5},{5... | collective-permute-start | bytes 122888 | tf_op jit(solution)/shard_map/ppermute | solution.py:71
  28.7 6.7 %collective-permute-start.1 = (bf16[16,1280]{1,0:T(8,128)(2,1)S(1)}, bf16[16,1280]{1,0:T(8,128)(2,1)S(1)}, u32[]{:S(2)}, u32[]{:S(2)}) collective-permute-start(bf16[16,1280]{1,0:T(8,128)(2,1)S(1)} %collective-permute-done), channel_id=1, source_target_pairs={{0,4},{4,8},{8,12},{12,16},{16,20},{20,24},{24,28},{28,0},{1,5},{5... | collective-permute-start | bytes 122888 | tf_op jit(solution)/shard_map/ppermute | solution.py:71
  35.4 6.7 %collective-permute-start.2 = (bf16[16,1280]{1,0:T(8,128)(2,1)S(1)}, bf16[16,1280]{1,0:T(8,128)(2,1)S(1)}, u32[]{:S(2)}, u32[]{:S(2)}) collective-permute-start(bf16[16,1280]{1,0:T(8,128)(2,1)S(1)} %collective-permute-done.1), channel_id=1, source_target_pairs={{0,4},{4,8},{8,12},{12,16},{16,20},{20,24},{24,28},{28,0},{1,5},{5... | collective-permute-start | bytes 122888 | tf_op jit(solution)/shard_map/ppermute | solution.py:71
  42.1 6.7 %collective-permute-start.3 = (bf16[16,1280]{1,0:T(8,128)(2,1)S(1)}, bf16[16,1280]{1,0:T(8,128)(2,1)S(1)}, u32[]{:S(2)}, u32[]{:S(2)}) collective-permute-start(bf16[16,1280]{1,0:T(8,128)(2,1)S(1)} %collective-permute-done.2), channel_id=1, source_target_pairs={{0,4},{4,8},{8,12},{12,16},{16,20},{20,24},{24,28},{28,0},{1,5},{5... | collective-permute-start | bytes 122888 | tf_op jit(solution)/shard_map/ppermute | solution.py:71
  48.8 7.0 %collective-permute-start.4 = (bf16[16,1280]{1,0:T(8,128)(2,1)S(1)}, bf16[16,1280]{1,0:T(8,128)(2,1)S(1)}, u32[]{:S(2)}, u32[]{:S(2)}) collective-permute-start(bf16[16,1280]{1,0:T(8,128)(2,1)S(1)} %collective-permute-done.3), channel_id=1, source_target_pairs={{0,4},{4,8},{8,12},{12,16},{16,20},{20,24},{24,28},{28,0},{1,5},{5... | collective-permute-start | bytes 122888 | tf_op jit(solution)/shard_map/ppermute | solution.py:71
  55.8 6.7 %collective-permute-start.5 = (bf16[16,1280]{1,0:T(8,128)(2,1)S(1)}, bf16[16,1280]{1,0:T(8,128)(2,1)S(1)}, u32[]{:S(2)}, u32[]{:S(2)}) collective-permute-start(bf16[16,1280]{1,0:T(8,128)(2,1)S(1)} %collective-permute-done.4), channel_id=1, source_target_pairs={{0,4},{4,8},{8,12},{12,16},{16,20},{20,24},{24,28},{28,0},{1,5},{5... | collective-permute-start | bytes 122888 | tf_op jit(solution)/shard_map/ppermute | solution.py:71
  57.0 77.0 %copy-start.4 = (s32[16]{0:T(128)S(1)}, s32[16]{0:T(128)}, u32[]{:S(2)}) copy-start(s32[16]{0:T(128)} %param.15) | copy-start | bytes 196
  62.5 6.7 %collective-permute-start.6 = (bf16[16,1280]{1,0:T(8,128)(2,1)S(1)}, bf16[16,1280]{1,0:T(8,128)(2,1)S(1)}, u32[]{:S(2)}, u32[]{:S(2)}) collective-permute-start(bf16[16,1280]{1,0:T(8,128)(2,1)S(1)} %collective-permute-done.5), channel_id=1, source_target_pairs={{0,4},{4,8},{8,12},{12,16},{16,20},{20,24},{24,28},{28,0},{1,5},{5... | collective-permute-start | bytes 122888 | tf_op jit(solution)/shard_map/ppermute | solution.py:71
  79.8 70.8 %copy-start.1 = (f32[384,1280]{1,0:T(8,128)}, f32[384,1280]{1,0:T(8,128)S(1)}, u32[]{:S(2)}) copy-start(f32[384,1280]{1,0:T(8,128)S(1)} %get-tuple-element.12) | copy-start | bytes 5898244
  112.0 38.6 %copy-start.3 = (f32[16]{0:T(128)}, f32[16]{0:T(128)S(1)}, u32[]{:S(2)}) copy-start(f32[16]{0:T(128)S(1)} %get-tuple-element.8) | copy-start | bytes 196
  136.3 10.9 %all-to-all-start = ((bf16[16,8,640]{2,0,1:T(8,128)(2,1)}), bf16[16,8,640]{2,0,1:T(8,128)(2,1)S(1)}, u32[]{:S(2)}, u32[]{:S(2)}) async-start(bf16[16,8,640]{2,0,1:T(8,128)(2,1)} %bitcast.15), calls=%async_computation.1 | async-start | bytes 327680 | tf_op jit(solution)/shard_map/all_to_all | solution.py:68
Sparse Core Ops, SparseCore 0:
  20.0 45.4 reduce-scatter.1
